TPU v7x, 256 devices: a whole 4x4x8 slice. The times are simulated.
256 devices in a mesh: tm: 32 (over y, z), row: 8 (over x, core).
Axes of the slice: x: 4, y: 4, z: 8, core: 2. Of those that a mesh axis runs over, the one named last changes fastest.
Arguments:
- precisions: float32 [32, 1024, 1024], P('tm', 'row'), as said below
- couplings: float32 [32, 1024, 1024], P('tm', 'row'), as said below
- right_sides: float32 [32, 1024, 256], P('tm', 'row'), may hold values from -6 to 6
Outputs:
- pivot_blocks: float32 [32, 1024, 1024], P('tm', 'row')
- coupling_blocks: float32 [32, 1024, 1024], P('tm', 'row')
- reduced_sides: float32 [32, 1024, 256], P('tm', 'row')
Inputs may be any that keep to these rules, and one draw needn't show every extreme that they name: precisions and couplings together form a symmetric positive definite block-tridiagonal matrix whose eigenvalues are 1 or more; couplings[0] is zero. `couplings`: see precisions.
All inputs are finite; a program needn't handle non-finite values.
Results may differ from a plain program's by a relative error of at most 0.00023.
Values sent between devices are 32-bit elements; how exact they have to be, the bound alone decides.
No kernel may reach another device: no remote copies, remote signals or barrier semaphores. Data moves between devices by JAX's collectives and lax.ppermute only.
A program may use at most 128 MiB of HBM per device.

v0:
```python
import jax
import jax.numpy as jnp
from jax import lax
from jax.sharding import PartitionSpec as P

LEVELS = 2


def from_behind(block, axis, distance):
    devices = range(lax.axis_size(axis))
    route = [(i - distance, i) for i in devices if i - distance in devices]
    return lax.ppermute(block, axis, route)


def contract(left, right):
    return lax.dot_general(left, right, (((0,), (0,)), ((), ())), precision=lax.Precision.HIGHEST)


def split_cholesky(matrix):
    order = matrix.shape[0]
    if order <= 512:
        return jnp.linalg.cholesky(matrix)
    half = order // 2
    upper_factor = split_cholesky(matrix[:half, :half])
    solved_cols = jax.scipy.linalg.solve_triangular(upper_factor, matrix[:half, half:], lower=True)
    lower_left = solved_cols.T
    remainder = matrix[half:, half:] - contract(solved_cols, solved_cols)
    lower_factor = split_cholesky(remainder)
    top_rows = jnp.concatenate(
        [upper_factor, jnp.zeros((half, order - half), matrix.dtype)], axis=1
    )
    bottom_rows = jnp.concatenate([lower_left, lower_factor], axis=1)
    return jnp.concatenate([top_rows, bottom_rows], axis=0)


def local(precisions, couplings, right_sides):
    diagonal_pivot_rows = precisions[0]
    offdiag_coupling_rows = couplings[0]
    rhs_side_rows = right_sides[0]
    row_count = diagonal_pivot_rows.shape[0]
    block_position = lax.axis_index("tm")
    row_start = lax.axis_index("row") * row_count
    offdiag_coupling_rows = jnp.where(
        block_position == 0, jnp.zeros_like(offdiag_coupling_rows), offdiag_coupling_rows
    )
    for level_step in range(LEVELS):
        level_stride = 1 << level_step
        whole_pivot, whole_coupling, whole_side = (
            lax.all_gather(diagonal_pivot_rows, "row", axis=0, tiled=True),
            lax.all_gather(offdiag_coupling_rows, "row", axis=0, tiled=True),
            lax.all_gather(rhs_side_rows, "row", axis=0, tiled=True),
        )
        next_coupling = from_behind(whole_coupling, "tm", -level_stride)
        factor = split_cholesky(whole_pivot)
        left_part = jax.scipy.linalg.cho_solve((factor, True), offdiag_coupling_rows.T)
        right_cols = lax.dynamic_slice_in_dim(next_coupling, row_start, row_count, 1)
        right_part = jax.scipy.linalg.cho_solve((factor, True), right_cols)
        left_block = lax.dot_general(
            left_part, whole_coupling, (((0,), (1,)), ((), ())), precision=lax.Precision.HIGHEST
        )
        left_side = contract(left_part, whole_side)
        right_block = contract(right_part, next_coupling)
        right_side = contract(right_part, whole_side)
        new_coupling = -contract(left_part, next_coupling)
        received_following = from_behind((left_block, left_side), "tm", -level_stride)
        received_previous = from_behind((right_block, right_side, new_coupling), "tm", level_stride)
        diagonal_pivot_rows = diagonal_pivot_rows - received_following[0] - received_previous[0]
        rhs_side_rows = rhs_side_rows - received_following[1] - received_previous[1]
        offdiag_coupling_rows = received_previous[2]
    return (diagonal_pivot_rows[None], offdiag_coupling_rows[None], rhs_side_rows[None])


def solution(mesh):
    placed = (P("tm", "row", None), P("tm", "row", None), P("tm", "row", None))
    return jax.shard_map(
        local,
        mesh=mesh,
        in_specs=placed,
        out_specs=(P("tm", "row", None), P("tm", "row", None), P("tm", "row", None)),
        check_vma=False,
    )
```

profile of v0, /device:TPU:8, one launch (start us, length us, event | category | flops | bytes accessed | tf_op | source)
XLA Modules:
  0.0 1219.0 jit_solution(4765637610458641546)
XLA Ops:
  13.9 38.0 %all-gather.16.cloned.1.call-done = f32[1,1024,1024]{1,2,0:T(8,128)} async-done(((f32[1,128,1024]{1,2,0:T(8,128)}), f32[1,1024,1024]{1,2,0:T(8,128)}) %all-gather.16.cloned.1.call-update) | async-done | bytes 4194320 | tf_op jit(solution)/shard_map/all_gather | solution.py:49
  55.0 11.7 cholesky.462
  77.4 11.7 cholesky.481
  99.8 11.7 cholesky.502
  122.6 11.7 cholesky.519
  156.4 39.3 %custom-call.44 = f32[4,128,128]{1,2,0:T(8,128)S(1)} custom-call(f32[4,128,128]{2,1,0:T(8,128)S(1)} %get-tuple-element.46), custom_call_target="InvertDiagBlocksLowerTriangular" | custom-call | tf_op jit(solution)/shard_map/jit(_solve_triangular)/triangular_solve | solution.py:25
  213.0 11.7 cholesky.534
  240.0 13.2 %cholesky.553 = f32[128,128]{1,0:T(8,128)} custom-call(f32[128,128]{1,0:T(8,128)} %cholesky.763), custom_call_target="Cholesky" | custom-call | tf_op jit(solution)/shard_map/jit(cholesky)/cholesky | solution.py:22
  266.8 11.9 cholesky.574
  290.6 11.7 cholesky.591
  308.1 23.2 %while.13 = (s32[]{:T(128)}, f32[1024,1024]{1,0:T(8,128)}, s32[8,2]{0,1:T(2,128)S(1)}, f32[8,128,128]{2,1,0:T(8,128)S(1)}, s32[]{:T(128)}) while((s32[]{:T(128)}, f32[1024,1024]{1,0:T(8,128)}, s32[8,2]{0,1:T(2,128)S(1)}, f32[8,128,128]{2,1,0:T(8,128)S(1)}, s32[]{:T(128)}) %tuple.193), condition=%wide.while_cond.1, body=%wide.while_body.1.sunk | while | flops 2 | bytes 131181 | solution.py:55
  331.3 78.6 %custom-call.48 = f32[8,128,128]{1,2,0:T(8,128)S(1)} custom-call(f32[8,128,128]{2,1,0:T(8,128)S(1)} %get-tuple-element.47), custom_call_target="InvertDiagBlocksLowerTriangular" | custom-call | tf_op jit(solution)/shard_map/jit(_cho_solve)/triangular_solve | solution.py:55
  440.3 66.3 %collective-permute-done.1 = f32[1024,1024]{1,0:T(8,128)S(1)} collective-permute-done((f32[1024,1024]{1,0:T(8,128)}, f32[1024,1024]{1,0:T(8,128)S(1)}, u32[]{:S(2)}, u32[]{:S(2)}) %collective-permute-start.1) | collective-permute-done | bytes 4194336 | tf_op jit(solution)/shard_map/ppermute | solution.py:12
  527.6 14.7 %collective-permute-done.2 = f32[128,1024]{0,1:T(8,128)S(1)} collective-permute-done((f32[128,1024]{0,1:T(8,128)S(1)}, f32[128,1024]{0,1:T(8,128)S(1)}, u32[]{:S(2)}, u32[]{:S(2)}) %collective-permute-start.2) | collective-permute-done | bytes 524320 | tf_op jit(solution)/shard_map/ppermute | solution.py:12
  549.8 14.0 %collective-permute-done.3 = f32[128,1024]{1,0:T(8,128)S(1)} collective-permute-done((f32[128,1024]{1,0:T(8,128)S(1)}, f32[128,1024]{1,0:T(8,128)S(1)}, u32[]{:S(2)}, u32[]{:S(2)}) %collective-permute-start.3) | collective-permute-done | bytes 524320 | tf_op jit(solution)/shard_map/ppermute | solution.py:12
  584.0 11.7 cholesky.606
  606.4 11.7 cholesky.625
  653.2 11.7 cholesky.663
  676.2 39.3 %custom-call.53 = f32[4,128,128]{1,2,0:T(8,128)S(1)} custom-call(f32[4,128,128]{2,1,0:T(8,128)S(1)} %get-tuple-element.49), custom_call_target="InvertDiagBlocksLowerTriangular" | custom-call | tf_op jit(solution)/shard_map/jit(_solve_triangular)/triangular_solve | solution.py:25
  758.8 13.2 %cholesky.697 = f32[128,128]{1,0:T(8,128)} custom-call(f32[128,128]{1,0:T(8,128)} %cholesky.789), custom_call_target="Cholesky" | custom-call | tf_op jit(solution)/shard_map/jit(cholesky)/cholesky | solution.py:22
  785.5 12.1 cholesky.718
  827.1 22.7 %while.15 = (s32[]{:T(128)}, f32[1024,1024]{1,0:T(8,128)}, s32[8,2]{0,1:T(2,128)S(1)}, f32[8,128,128]{2,1,0:T(8,128)S(1)}, s32[]{:T(128)}) while((s32[]{:T(128)}, f32[1024,1024]{1,0:T(8,128)}, s32[8,2]{0,1:T(2,128)S(1)}, f32[8,128,128]{2,1,0:T(8,128)S(1)}, s32[]{:T(128)}) %tuple.216), condition=%wide.while_cond.1.clone.1, body=%wide.while_body.1.clone.1.sunk | while | flops 2 | bytes 131181 | solution.py:55
  849.8 78.8 %custom-call.57 = f32[8,128,128]{1,2,0:T(8,128)S(1)} custom-call(f32[8,128,128]{2,1,0:T(8,128)S(1)} %get-tuple-element.50), custom_call_target="InvertDiagBlocksLowerTriangular" | custom-call | tf_op jit(solution)/shard_map/jit(_cho_solve)/triangular_solve | solution.py:55
  977.8 174.4 %collective-permute-done.5 = f32[1024,1024]{1,0:T(8,128)} collective-permute-done((f32[1024,1024]{1,0:T(8,128)}, f32[1024,1024]{1,0:T(8,128)}, u32[]{:S(2)}, u32[]{:S(2)}) %collective-permute-start.5) | collective-permute-done | bytes 4194336 | tf_op jit(solution)/shard_map/ppermute | solution.py:12
  (520 shorter events, 507.7 us)
Async XLA Ops:
  7.2 44.7 %all-gather.16.cloned.1.call-start = ((), (), s32[]{:S(2)}) async-start(), calls=%async_computation.3 | async-start | bytes 4718592 | tf_op jit(solution)/shard_map/all_gather | solution.py:49
  9.3 400.7 %all-gather.18.cloned.1.call-start = ((), (), s32[]{:S(2)}) async-start(), calls=%async_computation.4 | async-start | bytes 4718592 | tf_op jit(solution)/shard_map/all_gather | solution.py:50
  11.2 553.5 %all-gather.20.cloned.1.call-start = ((), (), s32[]{:S(2)}) async-start(), calls=%async_computation.5 | async-start | bytes 1179648 | tf_op jit(solution)/shard_map/all_gather | solution.py:51
  12.0 568.9 %all-gather.10.cloned.1.call-start = ((), (), s32[]{:S(2)}) async-start(), calls=%async_computation | async-start | bytes 4718592 | tf_op jit(solution)/shard_map/all_gather | solution.py:49
  305.5 110.1 %copy-start.15 = (f32[1024,128]{0,1:T(8,128)S(1)}, f32[1024,128]{0,1:T(8,128)}, u32[]{:S(2)}) copy-start(f32[1024,128]{0,1:T(8,128)} %fusion.497) | copy-start | bytes 1572868
  410.0 96.7 %collective-permute-start.1 = (f32[1024,1024]{1,0:T(8,128)}, f32[1024,1024]{1,0:T(8,128)S(1)}, u32[]{:S(2)}, u32[]{:S(2)}) collective-permute-start(f32[1024,1024]{1,0:T(8,128)} %bitcast.470), channel_id=1, source_target_pairs={{8,0},{16,8},{24,16},{32,24},{40,32},{48,40},{56,48},{64,56},{72,6... | collective-permute-start | bytes 12582920 | tf_op jit(solution)/shard_map/ppermute | solution.py:12
  437.0 90.6 %collective-permute-start = (f32[128,1024]{0,1:T(8,128)S(1)}, f32[128,1024]{0,1:T(8,128)S(1)}, u32[]{:S(2)}, u32[]{:S(2)}) collective-permute-start(f32[128,1024]{0,1:T(8,128)S(1)} %fusion.389), channel_id=1, source_target_pairs={{8,0},{16,8},{24,16},{32,24},{40,32},{48,40},{56,48},{64,56},{72,6... | collective-permute-start | bytes 1572872 | tf_op jit(solution)/shard_map/ppermute | solution.py:12
  525.1 17.3 %collective-permute-start.2 = (f32[128,1024]{0,1:T(8,128)S(1)}, f32[128,1024]{0,1:T(8,128)S(1)}, u32[]{:S(2)}, u32[]{:S(2)}) collective-permute-start(f32[128,1024]{0,1:T(8,128)S(1)} %fusion.395), channel_id=1, source_target_pairs={{0,8},{8,16},{16,24},{24,32},{32,40},{40,48},{48,56},{56,64},{64,7... | collective-permute-start | bytes 1572872 | tf_op jit(solution)/shard_map/ppermute | solution.py:12
  543.2 37.0 %copy-start.17 = (f32[1,128,256]{2,1,0:T(8,128)S(1)}, f32[1,128,256]{2,1,0:T(8,128)}, u32[]{:S(2)}) copy-start(f32[1,128,256]{2,1,0:T(8,128)} %param.10) | copy-start | bytes 393220
  543.2 408.4 %all-gather.12.cloned.1.call-start = ((), (), s32[]{:S(2)}) async-start(), calls=%async_computation.1 | async-start | bytes 4718592 | tf_op jit(solution)/shard_map/all_gather | solution.py:50
  547.9 16.0 %collective-permute-start.3 = (f32[128,1024]{1,0:T(8,128)S(1)}, f32[128,1024]{1,0:T(8,128)S(1)}, u32[]{:S(2)}, u32[]{:S(2)}) collective-permute-start(f32[128,1024]{1,0:T(8,128)S(1)} %convolution_negate_fusion.1), channel_id=1, source_target_pairs={{0,8},{8,16},{16,24},{24,32},{32,40},{40,48},{48,56},{56,64},{64,7... | collective-permute-start | bytes 1572872 | tf_op jit(solution)/shard_map/ppermute | solution.py:12
  564.7 398.9 %all-gather.14.cloned.1.call-start = ((), (), s32[]{:S(2)}) async-start(), calls=%async_computation.2 | async-start | bytes 1179648 | tf_op jit(solution)/shard_map/all_gather | solution.py:51
  567.0 8.3 collective-permute-start.8
  571.2 9.0 collective-permute-start.9
  827.1 111.4 %copy-start.14 = (f32[128,1024]{1,0:T(8,128)S(1)}, f32[128,1024]{1,0:T(8,128)}, u32[]{:S(2)}) copy-start(f32[128,1024]{1,0:T(8,128)} %copy-done.13) | copy-start | bytes 1572868
  951.6 200.6 %collective-permute-start.5 = (f32[1024,1024]{1,0:T(8,128)}, f32[1024,1024]{1,0:T(8,128)}, u32[]{:S(2)}, u32[]{:S(2)}) collective-permute-start(f32[1024,1024]{1,0:T(8,128)} %all-gather.12.cloned.1.call-done), channel_id=1, source_target_pairs={{16,0},{24,8},{32,16},{40,24},{48,32},{56,40},{64,48},{72,56},{80,... | collective-permute-start | bytes 12582920 | tf_op jit(solution)/shard_map/ppermute | solution.py:12
  963.6 189.8 %copy-start = (f32[1024,1024]{1,0:T(8,128)S(1)}, f32[1024,1024]{1,0:T(8,128)}, u32[]{:S(2)}) copy-start(f32[1024,1024]{1,0:T(8,128)} %get-tuple-element.457) | copy-start | bytes 12582916
  966.0 232.4 %collective-permute-start.10 = (f32[128,256]{1,0:T(8,128)S(1)}, f32[128,256]{1,0:T(8,128)S(1)}, u32[]{:S(2)}, u32[]{:S(2)}) collective-permute-start(f32[128,256]{1,0:T(8,128)S(1)} %fusion.398), channel_id=1, source_target_pairs={{16,0},{24,8},{32,16},{40,24},{48,32},{56,40},{64,48},{72,56},{80,... | collective-permute-start | bytes 393224 | tf_op jit(solution)/shard_map/ppermute | solution.py:12
  975.3 234.5 %collective-permute-start.4 = (f32[128,1024]{0,1:T(8,128)S(1)}, f32[128,1024]{0,1:T(8,128)S(1)}, u32[]{:S(2)}, u32[]{:S(2)}) collective-permute-start(f32[128,1024]{0,1:T(8,128)S(1)} %fusion.396), channel_id=1, source_target_pairs={{16,0},{24,8},{32,16},{40,24},{48,32},{56,40},{64,48},{72,56},{80,... | collective-permute-start | bytes 1572872 | tf_op jit(solution)/shard_map/ppermute | solution.py:12
  1175.1 34.0 %copy-start.16 = (f32[128,256]{1,0:T(8,128)S(1)}, f32[128,256]{1,0:T(8,128)}, u32[]{:S(2)}) copy-start(f32[128,256]{1,0:T(8,128)} %fusion.247) | copy-start | bytes 393220
  1175.2 34.7 %copy-start.4 = (f32[128,1024]{0,1:T(8,128)S(1)}, f32[128,1024]{0,1:T(8,128)}, u32[]{:S(2)}) copy-start(f32[128,1024]{0,1:T(8,128)} %fusion.33) | copy-start | bytes 1572868
  1175.2 34.7 %collective-permute-start.7 = (f32[128,1024]{1,0:T(8,128)S(1)}, f32[128,1024]{1,0:T(8,128)S(1)}, u32[]{:S(2)}, u32[]{:S(2)}) collective-permute-start(f32[128,1024]{1,0:T(8,128)S(1)} %convolution_negate_fusion), channel_id=1, source_target_pairs={{0,16},{8,24},{16,32},{24,40},{32,48},{40,56},{48,64},{56,72},{64,... | collective-permute-start | bytes 1572872 | tf_op jit(solution)/shard_map/ppermute | solution.py:12
  1189.1 20.7 %collective-permute-start.6 = (f32[128,1024]{0,1:T(8,128)S(1)}, f32[128,1024]{0,1:T(8,128)S(1)}, u32[]{:S(2)}, u32[]{:S(2)}) collective-permute-start(f32[128,1024]{0,1:T(8,128)S(1)} %fusion.397), channel_id=1, source_target_pairs={{0,16},{8,24},{16,32},{24,40},{32,48},{40,56},{48,64},{56,72},{64,... | collective-permute-start | bytes 1572872 | tf_op jit(solution)/shard_map/ppermute | solution.py:12
  1194.2 15.0 %collective-permute-start.11 = (f32[128,256]{1,0:T(8,128)S(1)}, f32[128,256]{1,0:T(8,128)S(1)}, u32[]{:S(2)}, u32[]{:S(2)}) collective-permute-start(f32[128,256]{1,0:T(8,128)S(1)} %fusion.399), channel_id=1, source_target_pairs={{0,16},{8,24},{16,32},{24,40},{32,48},{40,56},{48,64},{56,72},{64,... | collective-permute-start | bytes 393224 | tf_op jit(solution)/shard_map/ppermute | solution.py:12
  (16 other events, 101.1 us)
Sparse Core Ops, SparseCore 0:
  10.4 41.4 all-gather.15
  53.8 35.9 all-gather.17
  91.6 25.9 all-gather.19
  543.3 37.1 all-gather.9
  582.8 35.7 all-gather.11
  620.9 26.0 all-gather.13
where the time goes:
time: 1230 us; the launch traced here: 1220 us
  other arithmetic  586 us (48%)
  waiting for transfers between devices  324 us (26%)
  matrix products  156 us (13%)
  local copies, waits for them, and re-layouts  79.8 us (6%)
  starting transfers between devices  45.5 us (4%)
  between operations  27.1 us (2%)
    another operation x59, other arithmetic, split_cholesky(): return jnp.linalg.cholesky(matrix)  332 us
    ppermute x12, waiting for transfers between devices, from_behind(): return lax.ppermute(block, axis, route)  285 us
    another operation x5, other arithmetic, local(): jax.scipy.linalg.cho_solve((factor, True), offdiag_coupling_rows.T)  162 us
    another operation x5, other arithmetic, split_cholesky(): jax.scipy.linalg.solve_triangular(upper_factor, matrix[:half, half:], low...  79.2 us
    another operation x59, local copies, waits for them, and re-layouts, local(): jax.scipy.linalg.cho_solve((factor, True), offdiag_coupling_rows.T)  45.7 us
    another operation x60, matrix products, local(): jax.scipy.linalg.cho_solve((factor, True), offdiag_coupling_rows.T)  45.7 us
    ppermute x12, starting transfers between devices, from_behind(): return lax.ppermute(block, axis, route)  45.2 us
    dot_general x10, matrix products, contract(): lax.dot_general(left, right, (((0,), (0,)), ((), ())), precision=lax.Prec...  39.6 us
  transfers between devices with their start and end apart: 18, of which 7 were waited for; matrix products, arithmetic and copies ran while one was open for 67% of the time, Pallas kernels for 0%

commit v1 on v0

--- a/solution.py
+++ b/solution.py
@@ -4,6 +4,19 @@
 from jax.sharding import PartitionSpec as P
 
 LEVELS = 2
+
+
+def gather_around(x, axis, dim):
+    ways = lax.axis_size(axis)
+    up = [(d, (d + 1) % ways) for d in range(ways)]
+    down = [(d, (d - 1) % ways) for d in range(ways)]
+    earlier, later = ([x], [x])
+    for _ in range(ways // 2):
+        earlier.append(lax.ppermute(earlier[-1], axis, up))
+    for _ in range((ways - 1) // 2):
+        later.append(lax.ppermute(later[-1], axis, down))
+    line = jnp.concatenate([*earlier[::-1], *later[1:]], axis=dim)
+    return jnp.roll(line, (lax.axis_index(axis) - ways // 2) * x.shape[dim], axis=dim)
 
 
 def from_behind(block, axis, distance):
@@ -46,7 +59,7 @@
     for level_step in range(LEVELS):
         level_stride = 1 << level_step
         whole_pivot, whole_coupling, whole_side = (
-            lax.all_gather(diagonal_pivot_rows, "row", axis=0, tiled=True),
+            gather_around(diagonal_pivot_rows, "row", 0),
             lax.all_gather(offdiag_coupling_rows, "row", axis=0, tiled=True),
             lax.all_gather(rhs_side_rows, "row", axis=0, tiled=True),
         )

time: 1230 us -> 1290 us (1.049)
  waiting for transfers between devices: 324 us -> 351 us
  starting transfers between devices: 45.5 us -> 63.7 us
    ppermute x0 -> x14, waiting for transfers between devices: none -> 61.3 us  [the longest x8 51.8 us: gather_around(): earlier.append(lax.ppermute(earlier[-1], axis, up))]
    all_gather x2 -> x0, waiting for transfers between devices: 38 us -> none  [local(): lax.all_gather(diagonal_pivot_rows, 'row', axis=0, tiled=True)]
    ppermute x0 -> x14, starting transfers between devices: none -> 19.9 us  [the longest x6 14.8 us: gather_around(): later.append(lax.ppermute(later[-1], axis, down))]
    another operation x59, other arithmetic: 332 us -> 318 us  [split_cholesky(): return jnp.linalg.cholesky(matrix)]
  transfers between devices with their start and end apart: 18 -> 30, of which waited for: 7 -> 15; matrix products, arithmetic and copies ran while one was open for 67% -> 65% of each run, Pallas kernels for 0% -> 0%
where the time goes in v1:
time: 1290 us; the launch traced here: 1280 us
  other arithmetic  581 us (45%)
  waiting for transfers between devices  351 us (27%)
  matrix products  168 us (13%)
  local copies, waits for them, and re-layouts  89.6 us (7%)
  starting transfers between devices  63.7 us (5%)
  between operations  26.9 us (2%)
    another operation x59, other arithmetic, split_cholesky(): return jnp.linalg.cholesky(matrix)  318 us
    ppermute x12, waiting for transfers between devices, from_behind(): return lax.ppermute(block, axis, route)  289 us
    another operation x5, other arithmetic, local(): jax.scipy.linalg.cho_solve((factor, True), offdiag_coupling_rows.T)  165 us
    another operation x5, other arithmetic, split_cholesky(): jax.scipy.linalg.solve_triangular(upper_factor, matrix[:half, half:], low...  81.3 us
    ppermute x8, waiting for transfers between devices, gather_around(): earlier.append(lax.ppermute(earlier[-1], axis, up))  51.8 us
    another operation x60, matrix products, local(): jax.scipy.linalg.cho_solve((factor, True), offdiag_coupling_rows.T)  49.9 us
    another operation x59, local copies, waits for them, and re-layouts, local(): jax.scipy.linalg.cho_solve((factor, True), offdiag_coupling_rows.T)  46.6 us
    ppermute x12, starting transfers between devices, from_behind(): return lax.ppermute(block, axis, route)  43.4 us
  transfers between devices with their start and end apart: 30, of which 15 were waited for; matrix products, arithmetic and copies ran while one was open for 65% of the time, Pallas kernels for 0%

profile of v1, /device:TPU:8, one launch (start us, length us, event | category | flops | bytes accessed | tf_op | source)
XLA Modules:
  0.0 1280.4 jit_solution(72083442117897560)
XLA Ops:
  39.8 12.3 collective-permute-done.2
  68.9 11.7 cholesky.462
  91.2 12.1 cholesky.481
  113.9 11.7 cholesky.502
  136.7 11.9 cholesky.519
  153.9 11.9 while.12
  165.7 39.3 %custom-call.44 = f32[4,128,128]{1,2,0:T(8,128)S(1)} custom-call(f32[4,128,128]{2,1,0:T(8,128)S(1)} %get-tuple-element.47), custom_call_target="InvertDiagBlocksLowerTriangular" | custom-call | tf_op jit(solution)/shard_map/jit(_solve_triangular)/triangular_solve | solution.py:38
  224.8 11.7 cholesky.534
  249.8 11.7 cholesky.553
  274.3 11.9 cholesky.574
  298.2 11.7 cholesky.591
  317.0 23.4 %while.13 = (s32[]{:T(128)}, f32[1024,1024]{1,0:T(8,128)}, s32[8,2]{0,1:T(2,128)S(1)}, f32[8,128,128]{2,1,0:T(8,128)S(1)}, s32[]{:T(128)}) while((s32[]{:T(128)}, f32[1024,1024]{1,0:T(8,128)}, s32[8,2]{0,1:T(2,128)S(1)}, f32[8,128,128]{2,1,0:T(8,128)S(1)}, s32[]{:T(128)}) %tuple.194), condition=%wide.while_cond.1, body=%wide.while_body.1.sunk | while | flops 2 | bytes 131181 | solution.py:68
  340.4 78.8 %custom-call.48 = f32[8,128,128]{1,2,0:T(8,128)S(1)} custom-call(f32[8,128,128]{2,1,0:T(8,128)S(1)} %get-tuple-element.48), custom_call_target="InvertDiagBlocksLowerTriangular" | custom-call | tf_op jit(solution)/shard_map/jit(_cho_solve)/triangular_solve | solution.py:68
  461.0 77.4 %collective-permute-done.8 = f32[1024,1024]{1,0:T(8,128)S(1)} collective-permute-done((f32[1024,1024]{1,0:T(8,128)}, f32[1024,1024]{1,0:T(8,128)S(1)}, u32[]{:S(2)}, u32[]{:S(2)}) %collective-permute-start.8) | collective-permute-done | bytes 4194336 | tf_op jit(solution)/shard_map/ppermute | solution.py:25
  646.2 11.7 cholesky.606
  668.6 12.1 cholesky.625
  692.5 11.7 cholesky.646
  715.4 11.9 cholesky.663
  743.4 39.3 %custom-call.53 = f32[4,128,128]{1,2,0:T(8,128)S(1)} custom-call(f32[4,128,128]{2,1,0:T(8,128)S(1)} %get-tuple-element.50), custom_call_target="InvertDiagBlocksLowerTriangular" | custom-call | tf_op jit(solution)/shard_map/jit(_solve_triangular)/triangular_solve | solution.py:38
  802.4 11.7 cholesky.678
  851.9 11.9 cholesky.718
  894.7 23.4 %while.15 = (s32[]{:T(128)}, f32[1024,1024]{1,0:T(8,128)}, s32[8,2]{0,1:T(2,128)S(1)}, f32[8,128,128]{2,1,0:T(8,128)S(1)}, s32[]{:T(128)}) while((s32[]{:T(128)}, f32[1024,1024]{1,0:T(8,128)}, s32[8,2]{0,1:T(2,128)S(1)}, f32[8,128,128]{2,1,0:T(8,128)S(1)}, s32[]{:T(128)}) %tuple.213), condition=%wide.while_cond.1.clone.1, body=%wide.while_body.1.clone.1.sunk | while | flops 2 | bytes 131181 | solution.py:68
  918.2 78.8 %custom-call.57 = f32[8,128,128]{1,2,0:T(8,128)S(1)} custom-call(f32[8,128,128]{2,1,0:T(8,128)S(1)} %get-tuple-element.51), custom_call_target="InvertDiagBlocksLowerTriangular" | custom-call | tf_op jit(solution)/shard_map/jit(_cho_solve)/triangular_solve | solution.py:68
  1040.4 174.9 %collective-permute-done.19 = f32[1024,1024]{1,0:T(8,128)} collective-permute-done((f32[1024,1024]{1,0:T(8,128)}, f32[1024,1024]{1,0:T(8,128)}, u32[]{:S(2)}, u32[]{:S(2)}) %collective-permute-start.19) | collective-permute-done | bytes 4194336 | tf_op jit(solution)/shard_map/ppermute | solution.py:25
  (548 shorter events, 598.3 us)
Async XLA Ops:
  7.2 431.6 %all-gather.11.cloned.1.call-start = ((), (), s32[]{:S(2)}) async-start(), calls=%async_computation.2 | async-start | bytes 4718592 | tf_op jit(solution)/shard_map/all_gather | solution.py:63
  9.1 600.9 %all-gather.13.cloned.1.call-start = ((), (), s32[]{:S(2)}) async-start(), calls=%async_computation.3 | async-start | bytes 1179648 | tf_op jit(solution)/shard_map/all_gather | solution.py:64
  20.2 10.9 collective-permute-start.1
  20.3 16.1 %collective-permute-start.4 = (f32[128,1024]{0,1:T(8,128)S(1)}, f32[128,1024]{0,1:T(8,128)S(1)}, u32[]{:S(2)}, u32[]{:S(2)}) collective-permute-start(f32[128,1024]{0,1:T(8,128)S(1)} %bitcast.466), channel_id=1, source_target_pairs={{0,7},{1,0},{2,1},{3,2},{4,3},{5,4},{6,5},{7,6},{8,15},{9,8},{10,9... | collective-permute-start | bytes 1572872 | tf_op jit(solution)/shard_map/ppermute | solution.py:17
  31.1 21.0 %collective-permute-start.2 = (f32[128,1024]{0,1:T(8,128)S(1)}, f32[128,1024]{0,1:T(8,128)S(1)}, u32[]{:S(2)}, u32[]{:S(2)}) collective-permute-start(f32[128,1024]{0,1:T(8,128)S(1)} %collective-permute-done.1), channel_id=1, source_target_pairs={{0,1},{1,2},{2,3},{3,4},{4,5},{5,6},{6,7},{7,0},{8,9},{9,10},{10,1... | collective-permute-start | bytes 1572872 | tf_op jit(solution)/shard_map/ppermute | solution.py:15
  36.3 17.8 %collective-permute-start.5 = (f32[128,1024]{0,1:T(8,128)S(1)}, f32[128,1024]{0,1:T(8,128)S(1)}, u32[]{:S(2)}, u32[]{:S(2)}) collective-permute-start(f32[128,1024]{0,1:T(8,128)S(1)} %collective-permute-done.4), channel_id=1, source_target_pairs={{0,7},{1,0},{2,1},{3,2},{4,3},{5,4},{6,5},{7,6},{8,15},{9,8},{10,9... | collective-permute-start | bytes 1572872 | tf_op jit(solution)/shard_map/ppermute | solution.py:17
  52.2 964.5 %all-gather.7.cloned.1.call-start = ((), (), s32[]{:S(2)}) async-start(), calls=%async_computation | async-start | bytes 4718592 | tf_op jit(solution)/shard_map/all_gather | solution.py:63
  438.8 99.6 %collective-permute-start.8 = (f32[1024,1024]{1,0:T(8,128)}, f32[1024,1024]{1,0:T(8,128)S(1)}, u32[]{:S(2)}, u32[]{:S(2)}) collective-permute-start(f32[1024,1024]{1,0:T(8,128)} %bitcast.467), channel_id=1, source_target_pairs={{8,0},{16,8},{24,16},{32,24},{40,32},{48,40},{56,48},{64,56},{72,6... | collective-permute-start | bytes 12582920 | tf_op jit(solution)/shard_map/ppermute | solution.py:25
  458.1 117.7 %collective-permute-start.7 = (f32[128,1024]{0,1:T(8,128)S(1)}, f32[128,1024]{0,1:T(8,128)}, u32[]{:S(2)}, u32[]{:S(2)}) collective-permute-start(f32[128,1024]{0,1:T(8,128)S(1)} %fusion.394), channel_id=1, source_target_pairs={{8,0},{16,8},{24,16},{32,24},{40,32},{48,40},{56,48},{64,56},{72,6... | collective-permute-start | bytes 1572872 | tf_op jit(solution)/shard_map/ppermute | solution.py:25
  545.7 13.5 %collective-permute-start.17 = (f32[128,1024]{1,0:T(8,128)S(1)}, f32[128,1024]{1,0:T(8,128)S(1)}, u32[]{:S(2)}, u32[]{:S(2)}) collective-permute-start(f32[128,1024]{1,0:T(8,128)S(1)} %convolution_negate_fusion.1), channel_id=1, source_target_pairs={{0,8},{8,16},{16,24},{24,32},{32,40},{40,48},{48,56},{56,64},{64,7... | collective-permute-start | bytes 1572872 | tf_op jit(solution)/shard_map/ppermute | solution.py:25
  560.1 465.1 %all-gather.9.cloned.1.call-start = ((), (), s32[]{:S(2)}) async-start(), calls=%async_computation.1 | async-start | bytes 1179648 | tf_op jit(solution)/shard_map/all_gather | solution.py:64
  573.9 13.2 %collective-permute-start.9 = (f32[128,1024]{0,1:T(8,128)S(1)}, f32[128,1024]{0,1:T(8,128)S(1)}, u32[]{:S(2)}, u32[]{:S(2)}) collective-permute-start(f32[128,1024]{0,1:T(8,128)S(1)} %fusion.400), channel_id=1, source_target_pairs={{0,8},{8,16},{16,24},{24,32},{32,40},{40,48},{48,56},{56,64},{64,7... | collective-permute-start | bytes 1572872 | tf_op jit(solution)/shard_map/ppermute | solution.py:25
  588.2 10.2 collective-permute-start.10
  601.5 14.8 %collective-permute-start.14 = (f32[128,1024]{0,1:T(8,128)S(1)}, f32[128,1024]{0,1:T(8,128)S(1)}, u32[]{:S(2)}, u32[]{:S(2)}) collective-permute-start(f32[128,1024]{0,1:T(8,128)S(1)} %subtract_subtract_fusion), channel_id=1, source_target_pairs={{0,7},{1,0},{2,1},{3,2},{4,3},{5,4},{6,5},{7,6},{8,15},{9,8},{10,9... | collective-permute-start | bytes 1572872 | tf_op jit(solution)/shard_map/ppermute | solution.py:17
  608.1 10.8 collective-permute-start.12
  613.0 11.7 collective-permute-start.22
  616.3 15.5 %collective-permute-start.15 = (f32[128,1024]{0,1:T(8,128)S(1)}, f32[128,1024]{0,1:T(8,128)S(1)}, u32[]{:S(2)}, u32[]{:S(2)}) collective-permute-start(f32[128,1024]{0,1:T(8,128)S(1)} %collective-permute-done.14), channel_id=1, source_target_pairs={{0,7},{1,0},{2,1},{3,2},{4,3},{5,4},{6,5},{7,6},{8,15},{9,8},{10,9... | collective-permute-start | bytes 1572872 | tf_op jit(solution)/shard_map/ppermute | solution.py:17
  619.0 15.5 %collective-permute-start.13 = (f32[128,1024]{0,1:T(8,128)}, f32[128,1024]{0,1:T(8,128)}, u32[]{:S(2)}, u32[]{:S(2)}) collective-permute-start(f32[128,1024]{0,1:T(8,128)} %collective-permute-done.12), channel_id=1, source_target_pairs={{0,1},{1,2},{2,3},{3,4},{4,5},{5,6},{6,7},{7,0},{8,9},{9,10},{10,1... | collective-permute-start | bytes 1572872 | tf_op jit(solution)/shard_map/ppermute | solution.py:15
  1016.7 198.7 %collective-permute-start.19 = (f32[1024,1024]{1,0:T(8,128)}, f32[1024,1024]{1,0:T(8,128)}, u32[]{:S(2)}, u32[]{:S(2)}) collective-permute-start(f32[1024,1024]{1,0:T(8,128)} %all-gather.7.cloned.1.call-done), channel_id=1, source_target_pairs={{16,0},{24,8},{32,16},{40,24},{48,32},{56,40},{64,48},{72,56},{80,... | collective-permute-start | bytes 12582920 | tf_op jit(solution)/shard_map/ppermute | solution.py:25
  1027.6 232.9 %collective-permute-start.24 = (f32[128,256]{1,0:T(8,128)S(1)}, f32[128,256]{1,0:T(8,128)S(1)}, u32[]{:S(2)}, u32[]{:S(2)}) collective-permute-start(f32[128,256]{1,0:T(8,128)S(1)} %fusion.403), channel_id=1, source_target_pairs={{16,0},{24,8},{32,16},{40,24},{48,32},{56,40},{64,48},{72,56},{80,... | collective-permute-start | bytes 393224 | tf_op jit(solution)/shard_map/ppermute | solution.py:25
  1038.1 233.7 %collective-permute-start.18 = (f32[128,1024]{0,1:T(8,128)S(1)}, f32[128,1024]{0,1:T(8,128)S(1)}, u32[]{:S(2)}, u32[]{:S(2)}) collective-permute-start(f32[128,1024]{0,1:T(8,128)S(1)} %fusion.401), channel_id=1, source_target_pairs={{16,0},{24,8},{32,16},{40,24},{48,32},{56,40},{64,48},{72,56},{80,... | collective-permute-start | bytes 1572872 | tf_op jit(solution)/shard_map/ppermute | solution.py:25
  1238.2 33.6 %collective-permute-start.21 = (f32[128,1024]{1,0:T(8,128)S(1)}, f32[128,1024]{1,0:T(8,128)S(1)}, u32[]{:S(2)}, u32[]{:S(2)}) collective-permute-start(f32[128,1024]{1,0:T(8,128)S(1)} %convolution_negate_fusion), channel_id=1, source_target_pairs={{0,16},{8,24},{16,32},{24,40},{32,48},{40,56},{48,64},{56,72},{64,... | collective-permute-start | bytes 1572872 | tf_op jit(solution)/shard_map/ppermute | solution.py:25
  1249.6 22.2 %collective-permute-start.20 = (f32[128,1024]{0,1:T(8,128)S(1)}, f32[128,1024]{0,1:T(8,128)S(1)}, u32[]{:S(2)}, u32[]{:S(2)}) collective-permute-start(f32[128,1024]{0,1:T(8,128)S(1)} %fusion.402), channel_id=1, source_target_pairs={{0,16},{8,24},{16,32},{24,40},{32,48},{40,56},{48,64},{56,72},{64,... | collective-permute-start | bytes 1572872 | tf_op jit(solution)/shard_map/ppermute | solution.py:25
  1255.2 15.9 %collective-permute-start.25 = (f32[128,256]{1,0:T(8,128)S(1)}, f32[128,256]{1,0:T(8,128)S(1)}, u32[]{:S(2)}, u32[]{:S(2)}) collective-permute-start(f32[128,256]{1,0:T(8,128)S(1)} %fusion.404), channel_id=1, source_target_pairs={{0,16},{8,24},{16,32},{24,40},{32,48},{40,56},{48,64},{56,72},{64,... | collective-permute-start | bytes 393224 | tf_op jit(solution)/shard_map/ppermute | solution.py:25
  (22 other events, 629.1 us)
Sparse Core Ops, SparseCore 0:
  10.4 43.7 all-gather.10
  56.1 26.9 all-gather.12
  560.2 34.4 all-gather.6
  631.9 24.3 all-gather.8
